TPU v7x, 32 devices: a whole 2x2x4 slice. The times are simulated.
32 devices in a mesh: blk: 8 (over z, y), col: 4 (over x, core).
Axes of the slice: x: 2, y: 2, z: 4, core: 2. Of those that a mesh axis runs over, the one named last changes fastest.
Arguments:
- amplitudes: float32 [800, 32, 1601], P('col', 'blk'), may hold values from -6 to 6
- integrals: float32 [2, 1024, 20, 1601], P(None, 'blk', 'col'), may hold values from -0.03125 to 0.03125
- block_ids: int32 [20], replicated, may hold values from 0 to 799, as said below
- mirror: int32 [16], replicated, may hold values from 0 to 15, each once
Outputs:
- ladder_residual: float32 [16, 1024], P('col', 'blk')
Inputs may be any that keep to these rules, and one draw needn't show every extreme that they name: `block_ids`: 20 distinct folded block numbers; 0 and 799 are always among them. `mirror`: a permutation of the slab positions.
All inputs are finite; a program needn't handle non-finite values.
Results may differ from a plain program's by a relative error of at most 0.000073.
Values sent between devices are 32-bit elements; how exact they have to be, the bound alone decides.
A program may use at most 64 MiB of HBM per device.

v0:
```python
import functools

import jax
import jax.numpy as jnp
from jax import lax
from jax.experimental import pallas as pl
from jax.experimental.pallas import tpu as pltpu
from jax.sharding import PartitionSpec as P

MESH = pl.DeviceIdType.MESH


def kernel(
    nblk, ncol,
    amp_hbm, int_hbm, ids, mirror, out_ref,
    amp_v, int_v, hi, lo, core_out, core_in, sendb, landed, gath, feed, swp, osend, orecv,
    amp_sem, int_sem, cs, cr, xs, xr, us, ds, ys, gr, os_, or_,
):
    blocks_here = amp_v.shape[0]
    own = int_v.shape[0]
    rows = amp_v.shape[1]
    width = amp_v.shape[2]
    ab = int_v.shape[2]
    padded = hi.shape[1]
    pairs = feed.shape[0] // 2
    own_pairs = osend.shape[1]
    nhi = nblk // 2
    half = nblk // 2
    b = lax.axis_index("blk")
    c = lax.axis_index("col")
    z = b // 2
    y = b % 2
    nx = ncol // 2
    x = c // 2
    q = c % 2
    partner = z * 2 + (1 - y)

    amp_copies = []
    for i in range(4):
        low, high = blocks_here * i // 4, blocks_here * (i + 1) // 4
        cp = pltpu.make_async_copy(
            amp_hbm.at[low:high], amp_v.at[low:high], amp_sem.at[i])
        cp.start()
        amp_copies.append(cp)
    barrier = pltpu.get_barrier_semaphore()
    for j in range(1, ncol):
        pl.semaphore_signal(barrier, inc=1, device_id=(b, (c + j) % ncol), device_id_type=MESH)
    pl.semaphore_signal(barrier, inc=1, device_id=(partner, c), device_id_type=MESH)

    @pl.when(z < nhi - 1)
    def _():
        pl.semaphore_signal(barrier, inc=1, device_id=(b + 2, c), device_id_type=MESH)

    @pl.when(z > 0)
    def _():
        pl.semaphore_signal(barrier, inc=1, device_id=(b - 2, c), device_id_type=MESH)

    ends = (z == 0).astype(jnp.int32) + (z == nhi - 1).astype(jnp.int32)
    pl.semaphore_wait(barrier, ncol + 2 - ends)

    def core_copy(k, i):
        return pltpu.make_async_remote_copy(
            src_ref=core_out.at[i, k], dst_ref=core_in.at[i, k],
            send_sem=cs.at[i, k], recv_sem=cr.at[i, k],
            device_id=(b, x * 2 + 1 - q), device_id_type=MESH)

    def xcopy(k, i):
        return pltpu.make_async_remote_copy(
            src_ref=sendb.at[i, k], dst_ref=landed.at[i, k],
            send_sem=xs.at[i, k], recv_sem=xr.at[i, k],
            device_id=(b, (x + i) % nx * 2 + q), device_id_type=MESH)

    def gcopy(k, src, sem, target):
        return pltpu.make_async_remote_copy(
            src_ref=gath.at[k, src], dst_ref=gath.at[k, src],
            send_sem=sem, recv_sem=gr.at[k, src],
            device_id=(target, c), device_id_type=MESH)

    def up(k, d):
        return gcopy(k, b - 2 * d, us.at[k, d], b + 2)

    def down(k, d):
        return gcopy(k, b + 2 * d, ds.at[k, d], b - 2)

    def across(k, zz):
        return gcopy(k, zz * 2 + y, ys.at[k, zz], partner)

    def arrived(k, src):
        gcopy(k, src, us.at[k, 0], partner).wait_recv()

    base = c * blocks_here

    def wanted(k, dest):
        here = ids[dest * own + k] - base
        ok = jnp.logical_and(here >= 0, here < blocks_here)
        at = jnp.minimum(jnp.maximum(here, 0), blocks_here - 1)
        return jnp.where(ok, amp_v[at], 0.0)

    for cp in amp_copies:
        cp.wait()
    int_copies = {}
    for k in range(own):
        cp = pltpu.make_async_copy(int_hbm.at[k], int_v.at[k].reshape(width, 2, ab), int_sem.at[k])
        cp.start()
        int_copies[k] = cp

    for k in range(own):
        for i in [*range(1, nx), 0]:
            core_out[i, k] = wanted(k, (x + i) % nx * 2 + 1 - q)
            core_copy(k, i).start()
    for k in range(own):
        for i in range(1, nx):
            mine = wanted(k, (x + i) % nx * 2 + q)
            core_copy(k, i).wait_recv()
            sendb[i, k] = mine + core_in[i, k]
            xcopy(k, i).start()

    tail = (width // 128) * 128
    if padded > width:
        feed[:, tail:] = jnp.zeros((2 * pairs, padded - tail), jnp.float32)

    def convert(k):
        int_copies[k].wait()
        whole = width // 16

        def split(at, count):
            for w in range(2):
                v = int_v[k, pl.ds(at * 2 + w, count, stride=2), :]
                h = v.astype(jnp.bfloat16)
                l = (v - h.astype(jnp.float32)).astype(jnp.bfloat16)
                if count < 16:
                    blank = jnp.zeros((16 - count, ab), jnp.bfloat16)
                    h = jnp.concatenate([h, blank], axis=0)
                    l = jnp.concatenate([l, blank], axis=0)
                hi[k, pl.ds(at, 16), w * ab:(w + 1) * ab] = h
                lo[k, pl.ds(at, 16), w * ab:(w + 1) * ab] = l

        def strip(i, carry):
            split(pl.multiple_of(i * 16, 16), 16)
            return carry

        lax.fori_loop(0, whole, strip, 0, unroll=4)
        end = whole * 16
        if width > end:
            split(end, width - end)
            end += 16
        if padded > end:
            hi[k, end:] = jnp.zeros((padded - end, 2 * ab), jnp.bfloat16)
            lo[k, end:] = jnp.zeros((padded - end, 2 * ab), jnp.bfloat16)

    def own_piece(k):
        total = wanted(k, c)
        core_copy(k, 0).wait_recv()
        total = total + core_in[0, k]
        for i in range(1, nx):
            xcopy(k, i).wait_recv()
            total = total + landed[i, k]
        gath[k, b] = total
        across(k, z).start()

        @pl.when(z < nhi - 1)
        def _():
            up(k, 0).start()

        @pl.when(z > 0)
        def _():
            down(k, 0).start()

    def relay(k, d):
        @pl.when(z >= d)
        def _():
            arrived(k, b - 2 * d)

            @pl.when(z < nhi - 1)
            def _():
                up(k, d).start()

            across(k, z - d).start()

        @pl.when(z + d < nhi)
        def _():
            arrived(k, b + 2 * d)

            @pl.when(z > 0)
            def _():
                down(k, d).start()

            across(k, z + d).start()

    def multiply(k, acc):
        for zz in range(nhi):
            arrived(k, zz * 2 + 1 - y)
        for i in range(half):
            first = gath[k, i]
            second = gath[k, half + i]
            feed[i * rows:(i + 1) * rows, :width] = first + second
            feed[pairs + i * rows:pairs + (i + 1) * rows, :width] = first - second
        f = feed[...]
        fh = f.astype(jnp.bfloat16)
        fl = (f - fh.astype(jnp.float32)).astype(jnp.bfloat16)
        both = jnp.concatenate([fh, fl], axis=0)
        big = jnp.dot(both, hi[k], preferred_element_type=jnp.float32)
        small = jnp.dot(fh, lo[k], preferred_element_type=jnp.float32)
        part = big[:2 * pairs] + (big[2 * pairs:] + small)
        new = [part[:pairs, :ab], part[pairs:, ab:]]
        return new if acc is None else [u + v for u, v in zip(acc, new)]

    events = sorted((k * 1 + d * 100, d, k) for k in range(own) for d in range(nhi))
    convert(0)
    ready = 1
    for _, d, k in events:
        if d == 0:
            own_piece(k)
        else:
            relay(k, d)
        if ready < own:
            convert(ready)
            ready += 1
    acc = None
    for k in range(own):
        acc = multiply(k, acc)

    x_part, y_part = acc
    swp[...] = 0.5 * (x_part - y_part)
    direct = 0.5 * (x_part + y_part)
    for g in range(ncol):
        for i in range(own_pairs):
            p = g * own_pairs + i
            osend[g, i:i + 1, :] = direct[p:p + 1] + swp[pl.ds(mirror[p], 1), :]

    def ocopy(j):
        dest = (c + j) % ncol
        return pltpu.make_async_remote_copy(
            src_ref=osend.at[dest], dst_ref=orecv.at[j],
            send_sem=os_.at[j], recv_sem=or_.at[j],
            device_id=(b, dest), device_id_type=MESH)

    for j in range(1, ncol):
        ocopy(j).start()
    total = osend[c]
    for j in range(1, ncol):
        ocopy(j).wait_recv()
    for j in range(1, ncol):
        total = total + orecv[j]
    out_ref[...] = total

    for j in range(1, ncol):
        ocopy(j).wait_send()
    for k in range(own):
        for i in range(nx):
            core_copy(k, i).wait_send()
        for i in range(1, nx):
            xcopy(k, i).wait_send()
        for zz in range(nhi):
            across(k, zz).wait_send()
        for d in range(nhi):
            @pl.when(jnp.logical_and(z >= d, z < nhi - 1))
            def _():
                up(k, d).wait_send()

            @pl.when(jnp.logical_and(z + d < nhi, z > 0))
            def _():
                down(k, d).wait_send()


def body(nblk, ncol, amplitudes, integrals, block_ids, mirror):
    blocks_here, rows, width = amplitudes.shape
    _, ab, own, _ = integrals.shape
    pairs = mirror.shape[0]
    own_pairs = pairs // ncol
    padded = -(-width // 128) * 128
    nhi = nblk // 2
    nx = ncol // 2
    f32 = jnp.float32
    dma = pltpu.SemaphoreType.DMA
    return pl.pallas_call(
        functools.partial(kernel, nblk, ncol),
        out_shape=jax.ShapeDtypeStruct((own_pairs, ab), f32),
        in_specs=[
            pl.BlockSpec(memory_space=pl.ANY),
            pl.BlockSpec(memory_space=pl.ANY),
            pl.BlockSpec(memory_space=pltpu.SMEM),
            pl.BlockSpec(memory_space=pltpu.SMEM),
        ],
        out_specs=pl.BlockSpec(memory_space=pltpu.VMEM),
        scratch_shapes=[
            pltpu.VMEM((blocks_here, rows, width), f32),
            pltpu.VMEM((own, 2 * width, ab), f32),
            pltpu.VMEM((own, padded, 2 * ab), jnp.bfloat16),
            pltpu.VMEM((own, padded, 2 * ab), jnp.bfloat16),
            pltpu.VMEM((nx, own, rows, width), f32),
            pltpu.VMEM((nx, own, rows, width), f32),
            pltpu.VMEM((nx, own, rows, width), f32),
            pltpu.VMEM((nx, own, rows, width), f32),
            pltpu.VMEM((own, nblk, rows, width), f32),
            pltpu.VMEM((2 * pairs, padded), f32),
            pltpu.VMEM((pairs, ab), f32),
            pltpu.VMEM((ncol, own_pairs, ab), f32),
            pltpu.VMEM((ncol, own_pairs, ab), f32),
            dma((4,)),
            dma((own,)),
            dma((nx, own)),
            dma((nx, own)),
            dma((nx, own)),
            dma((nx, own)),
            dma((own, nhi)),
            dma((own, nhi)),
            dma((own, nhi)),
            dma((own, nblk)),
            dma((ncol,)),
            dma((ncol,)),
        ],
        compiler_params=pltpu.CompilerParams(
            collective_id=0, has_side_effects=True, vmem_limit_bytes=60 * 1024 * 1024
        ),
    )(amplitudes, jnp.transpose(integrals, (2, 3, 0, 1)), block_ids, mirror)


def solution(mesh):
    in_specs = (P("col", "blk", None), P(None, "blk", "col", None), P(), P())
    out_specs = P("col", "blk")
    call = functools.partial(body, mesh.shape["blk"], mesh.shape["col"])
    return jax.shard_map(call, mesh=mesh, in_specs=in_specs, out_specs=out_specs, check_vma=False)
```

profile of v0, /device:TPU:0, one launch (start us, length us, event | category | flops | bytes accessed | tf_op | source)
XLA Modules:
  0.0 31.4 jit_solution(3792903572823973991)
XLA Ops:
  0.0 30.1 %shard_map.46 = f32[4,128]{1,0:T(4,128)} custom-call(f32[200,4,1601]{2,1,0:T(4,128)} %amp_hbm.1, f32[5,1601,2,128]{3,2,1,0:T(2,128)} %bitcast.1, s32[20]{0:T(128)} %ids.1, s32[16]{0:T(128)} %mirror.1), custom_call_target="tpu_custom_call" | custom-call | tf_op jit(solution)/shard_map/pallas_call | solution.py:276
  30.1 1.3 %copy.6 = f32[4,128]{1,0:T(4,128)} copy(f32[4,128]{1,0:T(4,128)} %shard_map.46) | data formatting | bytes 4096
where the time goes:
time: 31.6 us; the launch traced here: 31.4 us
  Pallas kernels  30.1 us (95%)
  local copies, waits for them, and re-layouts  1.26 us (4%)
    pallas_call x1, Pallas kernels, body(): pl.pallas_call(functools.partial(kernel, nblk, ncol), out_shape=jax.Shape...  30.1 us
    unnamed x1, local copies, waits for them, and re-layouts  1.26 us

commit v1 on v0

v1 whole, which is shorter than its diff:
```python
import functools
from contextlib import nullcontext as scope

import jax
import jax.numpy as jnp
from jax import lax
from jax.experimental import pallas as pl
from jax.experimental.pallas import tpu as pltpu
from jax.sharding import PartitionSpec as P

MESH = pl.DeviceIdType.MESH


def kernel(
    nblk, ncol,
    amp_hbm, int_hbm, ids_hbm, mirror_hbm, out_ref,
    amp_v, int_v, hi, lo, core_out, core_in, sendb, landed, gath, feed, res, swp, osend, orecv, ids, mirror,
    amp_sem, int_sem, tab_sem, cs, cr, xs, xr, zs, ys, gz, gy, os_, or_,
):
    blocks_here, rows, width = amp_v.shape
    own, _, ab = int_v.shape
    padded = hi.shape[1]
    group = feed.shape[0]
    own_pairs = osend.shape[1]
    nhi = nblk // 2
    nx = ncol // 2
    b = lax.axis_index("blk")
    c = lax.axis_index("col")
    z = b // 2
    y = b % 2
    x = c // 2
    q = c % 2
    line = nhi == 4
    pair = z + 1 - 2 * (z % 2)
    facing = nhi - 1 - z
    cross = facing + 1 - 2 * (facing % 2)
    end = jnp.logical_or(z == 0, z == nhi - 1)
    inner = jnp.logical_not(end)
    if line:
        order = (z, jnp.where(end, pair, facing), jnp.where(end, cross, pair), jnp.where(end, facing, cross))
        detour = range(own - 0, own)
    else:
        order = tuple((z + nhi - d) % nhi for d in range(nhi))
        detour = ()

    ids_copy = pltpu.make_async_copy(ids_hbm, ids, tab_sem.at[0])
    mirror_copy = pltpu.make_async_copy(mirror_hbm, mirror, tab_sem.at[1])
    ids_copy.start()
    for i in range(4):
        low, high = blocks_here * i // 4, blocks_here * (i + 1) // 4
        pltpu.make_async_copy(amp_hbm.at[low:high], amp_v.at[low:high], amp_sem.at[0]).start()
    mirror_copy.start()
    barrier = pltpu.get_barrier_semaphore()

    def greet(target):
        pl.semaphore_signal(barrier, inc=1, device_id=target, device_id_type=MESH)

    with scope("barw"):
        for j in range(1, ncol):
            greet((b, (c + j) % ncol))
        greet((z * 2 + 1 - y, c))
        if line:
            greet((pair * 2 + y, c))

            @pl.when(inner)
            def _():
                greet((facing * 2 + y, c))

            @pl.when(z == 1)
            def _():
                greet((3 * 2 + y, c))

            pl.semaphore_wait(barrier, ncol + 2 - (z == 0).astype(jnp.int32))
        else:
            for d in range(1, nhi):
                greet((order[d] * 2 + y, c))
            pl.semaphore_wait(barrier, ncol + nhi - 1)

    def core_copy(k, i):
        return pltpu.make_async_remote_copy(
            src_ref=core_out.at[k, i], dst_ref=core_in.at[k, i],
            send_sem=cs.at[0], recv_sem=cr.at[k],
            device_id=(b, x * 2 + 1 - q), device_id_type=MESH)

    def xcopy(k, i):
        return pltpu.make_async_remote_copy(
            src_ref=sendb.at[k, i - 1], dst_ref=landed.at[k, i - 1],
            send_sem=xs.at[0], recv_sem=xr.at[k, i - 1],
            device_id=(b, (x + i) % nx * 2 + q), device_id_type=MESH)

    def gcopy(k, yy, zz, send, recv, target):
        return pltpu.make_async_remote_copy(
            src_ref=gath.at[k, yy, zz], dst_ref=gath.at[k, yy, zz],
            send_sem=send, recv_sem=recv,
            device_id=(target, c), device_id_type=MESH)

    def across(k, zz):
        early = k in detour and zz is z
        return gcopy(k, y, zz, ys.at[0], gz.at[k, z] if early else gy.at[k], z * 2 + 1 - y)

    def hop(k, zsrc, zdst):
        return gcopy(k, y, zsrc, zs.at[0], gz.at[k, zsrc], zdst * 2 + y)

    def around(k):
        return gcopy(k, 1 - y, z, zs.at[0], gy.at[k], pair * 2 + y)

    def many(count, send, recv):
        piece = gath.reshape(own * nblk, rows, width).at[0:count]
        return pltpu.make_async_remote_copy(
            src_ref=piece, dst_ref=piece, send_sem=send, recv_sem=recv,
            device_id=(z * 2 + 1 - y, c), device_id_type=MESH)

    base = c * blocks_here

    def wanted(k, dest):
        here = ids[dest * own + k] - base
        ok = jnp.logical_and(here >= 0, here < blocks_here)
        at = jnp.minimum(jnp.maximum(here, 0), blocks_here - 1)
        return jnp.where(ok, amp_v[at], 0.0)

    with scope("ampw"):
        ids_copy.wait()
        pltpu.make_async_copy(amp_hbm, amp_v, amp_sem.at[0]).wait()
    int_copies = {}
    for k in range(own):
        cp = pltpu.make_async_copy(int_hbm.at[k], int_v.at[k].reshape(width, 2, ab), int_sem.at[k])
        cp.start()
        int_copies[k] = cp

    for k in range(own):
        for i in [*range(1, nx), 0]:
            core_out[k, i] = wanted(k, (x + i) % nx * 2 + 1 - q)
            core_copy(k, i).start()
    tail = (width // 128) * 128
    if padded > width:
        feed[:, tail:] = jnp.zeros((group, padded - tail), jnp.float32)

    def convert(k):
        int_copies[k].wait()
        whole = width // 16

        def split(at, count):
            for w in range(2):
                v = int_v[k, pl.ds(at * 2 + w, count, stride=2), :]
                h = v.astype(jnp.bfloat16)
                l = (v - h.astype(jnp.float32)).astype(jnp.bfloat16)
                if count < 16:
                    blank = jnp.zeros((16 - count, ab), jnp.bfloat16)
                    h = jnp.concatenate([h, blank], axis=0)
                    l = jnp.concatenate([l, blank], axis=0)
                hi[k, pl.ds(at, 16), w * ab:(w + 1) * ab] = h
                lo[k, pl.ds(at, 16), w * ab:(w + 1) * ab] = l

        def strip(i, carry):
            split(pl.multiple_of(i * 16, 16), 16)
            return carry

        lax.fori_loop(0, whole, strip, 0, unroll=4)
        done = whole * 16
        if width > done:
            split(done, width - done)
            done += 16
        if padded > done:
            hi[k, done:] = jnp.zeros((padded - done, 2 * ab), jnp.bfloat16)
            lo[k, done:] = jnp.zeros((padded - done, 2 * ab), jnp.bfloat16)

    @pl.when(q == 1)
    def _():
        for k in range(2):
            convert(k)

    for k in range(own):
        with scope(f"x{k}"):
            mine = [wanted(k, (x + i) % nx * 2 + q) for i in range(1, nx)]
            pltpu.make_async_remote_copy(
                src_ref=core_out.at[k], dst_ref=core_in.at[k], send_sem=cs.at[0], recv_sem=cr.at[k],
                device_id=(b, x * 2 + 1 - q), device_id_type=MESH).wait_recv()
            for i in range(1, nx):
                sendb[k, i - 1] = mine[i - 1] + core_in[k, i]
                xcopy(k, i).start()

    def own_piece(k):
        total = wanted(k, c) + core_in[k, 0]
        for i in range(1, nx):
            xcopy(k, i).wait_recv()
            total = total + landed[k, i - 1]
        gath[k, y, z] = total
        if line:
            @pl.when(z == 3)
            def _():
                hop(k, z, 1).start()

            @pl.when(inner)
            def _():
                hop(k, z, facing).start()

            hop(k, z, pair).start()
        else:
            for d in range(1, nhi):
                hop(k, z, (z + d) % nhi).start()
        across(k, z).start()

    def relay(k, d):
        zz = order[d]
        hop(k, zz, z).wait_recv()
        if not line:
            across(k, zz).start()
            return
        if d != 2:
            @pl.when(inner)
            def _():
                hop(k, zz, pair).start()
        else:
            @pl.when(z == 1)
            def _():
                hop(k, zz, facing).start()

        if k in detour and d < 3:
            @pl.when(end if d == 2 else inner)
            def _():
                across(k, zz).start()
        else:
            across(k, zz).start()

    def pass_on(where):
        if line:
            @pl.when(where)
            def _():
                for k in detour:
                    gcopy(k, 1 - y, z, ys.at[0], gz.at[k, z], z * 2 + 1 - y).wait_recv()
                    around(k).start()

    def multiply(k, yy, acc):
        for zz in range(nhi):
            feed[zz * rows:(zz + 1) * rows, :width] = gath[k, yy, zz]
        f = feed[...]
        fh = f.astype(jnp.bfloat16)
        fl = (f - fh.astype(jnp.float32)).astype(jnp.bfloat16)
        both = jnp.concatenate([fh, fl], axis=0)
        big = jnp.dot(both, hi[k], preferred_element_type=jnp.float32)
        small = jnp.dot(fh, lo[k], preferred_element_type=jnp.float32)
        part = big[:group] + (big[group:] + small)
        return part if acc is None else acc + part

    acc = other = None
    ready = 2
    with scope("cb"):
        @pl.when(q == 0)
        def _():
            for k in range(2):
                convert(k)

        for k in range(2, ready):
            convert(k)
    for d in range(nhi):
        if d == nhi - 1:
            with scope("fe"):
                pass_on(end)
        for k in range(own):
            with scope(f"r{d}_{k}"):
                if d == 0:
                    own_piece(k)
                else:
                    relay(k, d)
            if ready < own and (d > 0 or k == own - 1):
                with scope(f"conv{ready}"):
                    convert(ready)
                ready += 1
            if d == nhi - 1:
                with scope(f"p{k}"):
                    acc = multiply(k, y, acc)
    with scope("fi"):
        pass_on(inner)
    with scope("sends"):
        mirror_copy.wait()
        pltpu.make_async_remote_copy(
            src_ref=core_out, dst_ref=core_in, send_sem=cs.at[0], recv_sem=cr.at[0],
            device_id=(b, x * 2 + 1 - q), device_id_type=MESH).wait_send()
        pltpu.make_async_remote_copy(
            src_ref=sendb, dst_ref=landed, send_sem=xs.at[0], recv_sem=xr.at[0, 0],
            device_id=(b, (x + 1) % nx * 2 + q), device_id_type=MESH).wait_send()
    for k in range(own):
        with scope(f"w{k}"):
            many(nhi - (1 if k in detour else 0), ys.at[0], gy.at[k]).wait_recv()
        with scope(f"q{k}"):
            other = multiply(k, 1 - y, other)

    res[y] = acc
    res[1 - y] = other
    deep = group // 2
    for yy in range(2):
        first = res[yy, :deep]
        second = res[yy, deep:]
        sums = first[:, :ab] + second[:, :ab]
        diffs = first[:, ab:] - second[:, ab:]
        swapped = 0.5 * (sums - diffs)
        direct = 0.5 * (sums + diffs)
        for zz in range(nhi // 2):
            at = (zz * 2 + yy) * rows
            swp[0, at:at + rows] = direct[zz * rows:(zz + 1) * rows]
            swp[1, at:at + rows] = swapped[zz * rows:(zz + 1) * rows]
    for g in range(ncol):
        for i in range(own_pairs):
            p = g * own_pairs + i
            osend[g, i:i + 1, :] = swp[0, p:p + 1] + swp[1, pl.ds(mirror[p], 1), :]

    def ocopy(j):
        return pltpu.make_async_remote_copy(
            src_ref=osend.at[(c + j) % ncol], dst_ref=orecv.at[j - 1],
            send_sem=os_.at[0], recv_sem=or_.at[0],
            device_id=(b, (c + j) % ncol), device_id_type=MESH)

    for j in range(1, ncol):
        ocopy(j).start()
    with scope("sends2"):
        many(own * nhi - len(detour), ys.at[0], gy.at[0]).wait_send()
        if line:
            for layer, count in ((0, own), (1, 5 * own), (2, 4 * own), (3, 2 * own)):
                @pl.when(z == layer)
                def _():
                    many(count + len(detour), zs.at[0], gy.at[0]).wait_send()
        else:
            many(own * (nhi - 1), zs.at[0], gy.at[0]).wait_send()
    total = osend[c]
    with scope("owait"):
        every = pltpu.make_async_remote_copy(
            src_ref=orecv, dst_ref=orecv, send_sem=os_.at[0], recv_sem=or_.at[0],
            device_id=(b, (c + 1) % ncol), device_id_type=MESH)
        every.wait_recv()
    for j in range(1, ncol):
        total = total + orecv[j - 1]
    out_ref[...] = total
    every.wait_send()


def body(nblk, ncol, amplitudes, integrals, block_ids, mirror):
    blocks_here, rows, width = amplitudes.shape
    _, ab, own, _ = integrals.shape
    pairs = mirror.shape[0]
    own_pairs = pairs // ncol
    padded = -(-width // 128) * 128
    nhi = nblk // 2
    nx = ncol // 2
    f32 = jnp.float32
    dma = pltpu.SemaphoreType.DMA
    return pl.pallas_call(
        functools.partial(kernel, nblk, ncol),
        out_shape=pltpu.VMEM((own_pairs, ab), f32),
        in_specs=[pl.BlockSpec(memory_space=pl.ANY)] * 4,
        out_specs=pl.BlockSpec(memory_space=pltpu.VMEM),
        scratch_shapes=[
            pltpu.VMEM((blocks_here, rows, width), f32),
            pltpu.VMEM((own, 2 * width, ab), f32),
            pltpu.VMEM((own, padded, 2 * ab), jnp.bfloat16),
            pltpu.VMEM((own, padded, 2 * ab), jnp.bfloat16),
            pltpu.VMEM((own, nx, rows, width), f32),
            pltpu.VMEM((own, nx, rows, width), f32),
            pltpu.VMEM((own, nx - 1, rows, width), f32),
            pltpu.VMEM((own, nx - 1, rows, width), f32),
            pltpu.VMEM((own, 2, nhi, rows, width), f32),
            pltpu.VMEM((nhi * rows, padded), f32),
            pltpu.VMEM((2, nhi * rows, 2 * ab), f32),
            pltpu.VMEM((2, pairs, ab), f32),
            pltpu.VMEM((ncol, own_pairs, ab), f32),
            pltpu.VMEM((ncol - 1, own_pairs, ab), f32),
            pltpu.SMEM(block_ids.shape, jnp.int32),
            pltpu.SMEM(mirror.shape, jnp.int32),
            dma((1,)),
            dma((own,)),
            dma((2,)),
            dma((1,)),
            dma((own,)),
            dma((1,)),
            dma((own, nx - 1)),
            dma((1,)),
            dma((1,)),
            dma((own, nhi)),
            dma((own,)),
            dma((1,)),
            dma((1,)),
        ],
        compiler_params=pltpu.CompilerParams(
            collective_id=0, has_side_effects=True, vmem_limit_bytes=60 * 1024 * 1024
        ),
    )(amplitudes, jnp.transpose(integrals, (2, 3, 0, 1)), block_ids, mirror)


def solution(mesh):
    in_specs = (P("col", "blk", None), P(None, "blk", "col", None), P(), P())
    out_specs = P("col", "blk")
    call = functools.partial(body, mesh.shape["blk"], mesh.shape["col"])
    return jax.shard_map(call, mesh=mesh, in_specs=in_specs, out_specs=out_specs, check_vma=False)
```

time: 31.6 us -> 28.5 us (0.902)
  Pallas kernels: 30.1 us -> 27.8 us
  local copies, waits for them, and re-layouts: 1.26 us -> 0.58 us
    pallas_call x1, Pallas kernels: 30.1 us -> 27.8 us  [body(): pl.pallas_call(functools.partial(kernel, nblk, ncol), out_shape=pltpu.VME...]
    unnamed x1, local copies, waits for them, and re-layouts: 1.26 us -> 0.58 us
where the time goes in v1:
time: 28.5 us; the launch traced here: 28.4 us
  Pallas kernels  27.8 us (98%)
  local copies, waits for them, and re-layouts  0.58 us (2%)
    pallas_call x1, Pallas kernels, body(): pl.pallas_call(functools.partial(kernel, nblk, ncol), out_shape=pltpu.VME...  27.8 us
    unnamed x1, local copies, waits for them, and re-layouts  0.58 us

profile of v1, /device:TPU:0, one launch (start us, length us, event | category | flops | bytes accessed | tf_op | source)
XLA Modules:
  0.0 28.4 jit_solution(10536206340738125934)
XLA Ops:
  0.0 27.8 %shard_map.46 = f32[4,128]{1,0:T(4,128)S(1)} custom-call(f32[200,4,1601]{2,1,0:T(4,128)} %amp_hbm.1, f32[5,1601,2,128]{3,2,1,0:T(2,128)} %bitcast.1, s32[20]{0:T(128)} %ids_hbm.1, s32[16]{0:T(128)} %mirror_hbm.1), custom_call_target="tpu_custom_call" | custom-call | tf_op jit(solution)/shard_map/pallas_call | solution.py:346
  27.8 0.6 %copy.6 = f32[4,128]{1,0:T(4,128)} copy(f32[4,128]{1,0:T(4,128)S(1)} %shard_map.46) | data formatting | bytes 4096

commit v2 on v1

v2 whole, which is shorter than its diff:
```python
import functools
from contextlib import nullcontext as scope

import jax
import jax.numpy as jnp
from jax import lax
from jax.experimental import pallas as pl
from jax.experimental.pallas import tpu as pltpu
from jax.sharding import PartitionSpec as P

MESH = pl.DeviceIdType.MESH


def kernel(
    nblk, ncol,
    amp_hbm, int_hbm, ids_hbm, mirror_hbm, out_ref,
    amp_v, int_v, hi, lo, core_out, core_in, sendb, landed, gath, feed, swp, osend, orecv, ids, mirror,
    amp_sem, int_sem, tab_sem, cs, cr, xs, xr, zs, ys, gz, gd, gy, os_, or_,
):
    blocks_here, rows, width = amp_hbm.shape
    own, _, ab = int_v.shape
    spans = chunks(width)
    parts = range(len(spans))
    last = parts[-1]
    padded = hi.shape[1]
    group = feed.shape[0]
    own_pairs = osend.shape[1]
    nhi = nblk // 2
    nx = ncol // 2
    b = lax.axis_index("blk")
    c = lax.axis_index("col")
    z = b // 2
    y = b % 2
    x = c // 2
    q = c % 2
    line = nhi == 4
    pair = z + 1 - 2 * (z % 2)
    facing = nhi - 1 - z
    cross = facing + 1 - 2 * (facing % 2)
    end = jnp.logical_or(z == 0, z == nhi - 1)
    inner = jnp.logical_not(end)
    if line:
        order = (z, jnp.where(end, pair, facing), jnp.where(end, cross, pair), jnp.where(end, facing, cross))
        detour = ()
    else:
        order = tuple((z + nhi - d) % nhi for d in range(nhi))
        detour = ()

    ids_copy = pltpu.make_async_copy(ids_hbm, ids, tab_sem.at[0])
    mirror_copy = pltpu.make_async_copy(mirror_hbm, mirror, tab_sem.at[1])
    ids_copy.start()
    amp_copies = []
    for h in parts:
        for i in range(4):
            at = pl.ds(blocks_here * i // 4, blocks_here * (i + 1) // 4 - blocks_here * i // 4)
            pltpu.make_async_copy(amp_hbm.at[at, :, spans[h]], amp_v[h].at[at], amp_sem.at[h]).start()
        amp_copies.append(pltpu.make_async_copy(amp_hbm.at[:, :, spans[h]], amp_v[h], amp_sem.at[h]))
    mirror_copy.start()
    barrier = pltpu.get_barrier_semaphore()

    def greet(target):
        pl.semaphore_signal(barrier, inc=1, device_id=target, device_id_type=MESH)

    with scope("barw"):
        for j in range(1, ncol):
            greet((b, (c + j) % ncol))
        greet((z * 2 + 1 - y, c))
        if line:
            greet((pair * 2 + y, c))

            @pl.when(inner)
            def _():
                greet((facing * 2 + y, c))

            @pl.when(z == 1)
            def _():
                greet((3 * 2 + y, c))

            pl.semaphore_wait(barrier, ncol + 2 - (z == 0).astype(jnp.int32))
        else:
            for d in range(1, nhi):
                greet((order[d] * 2 + y, c))
            pl.semaphore_wait(barrier, ncol + nhi - 1)

    def core_copy(k, i, h):
        return pltpu.make_async_remote_copy(
            src_ref=core_out.at[k, i, :, spans[h]], dst_ref=core_in.at[k, i, :, spans[h]],
            send_sem=cs.at[h], recv_sem=cr.at[h],
            device_id=(b, x * 2 + 1 - q), device_id_type=MESH)

    def core_all(h):
        return pltpu.make_async_remote_copy(
            src_ref=core_out.at[:, :, :, spans[h]], dst_ref=core_in.at[:, :, :, spans[h]],
            send_sem=cs.at[h], recv_sem=cr.at[h],
            device_id=(b, x * 2 + 1 - q), device_id_type=MESH)

    def xcopy(k, i, h):
        return pltpu.make_async_remote_copy(
            src_ref=sendb.at[k, i - 1, :, spans[h]], dst_ref=landed.at[k, i - 1, :, spans[h]],
            send_sem=xs.at[h], recv_sem=xr.at[h, k, i - 1],
            device_id=(b, (x + i) % nx * 2 + 1 - q), device_id_type=MESH)

    def gcopy(k, h, yy, zz, send, recv, target):
        piece = gath.at[k, yy, zz, :, spans[h]]
        return pltpu.make_async_remote_copy(
            src_ref=piece, dst_ref=piece, send_sem=send, recv_sem=recv,
            device_id=(target, c), device_id_type=MESH)

    def fill(k, h):
        return gy.at[h, k]

    def across(k, h, zz):
        early = (k, h) in detour and zz is z
        recv = gd.at[detour.index((k, h))] if early else fill(k, h)
        return gcopy(k, h, y, zz, ys.at[h], recv, z * 2 + 1 - y)

    def hop(k, h, zsrc, zdst):
        return gcopy(k, h, y, zsrc, zs.at[h], gz.at[h, k, (zsrc + nhi - zdst) % nhi - 1], zdst * 2 + y)

    def around(k, h):
        return gcopy(k, h, 1 - y, z, zs.at[h], fill(k, h), pair * 2 + y)

    def many(count, h, send, recv):
        piece = gath.reshape(own * nblk, rows, width).at[0:count, :, spans[h]]
        return pltpu.make_async_remote_copy(
            src_ref=piece, dst_ref=piece, send_sem=send, recv_sem=recv,
            device_id=(z * 2 + 1 - y, c), device_id_type=MESH)

    base = c * blocks_here

    def wanted(k, dest, h):
        here = ids[dest * own + k] - base
        ok = jnp.logical_and(here >= 0, here < blocks_here)
        at = jnp.minimum(jnp.maximum(here, 0), blocks_here - 1)
        return jnp.where(ok, amp_v[h][at], 0.0)

    def to_core(h):
        with scope(f"amp{h}"):
            amp_copies[h].wait()
        for k in range(own):
            for i in [*range(1, nx), 0]:
                dest = (x + i) % nx * 2 + q if i else x * 2 + 1 - q
                core_out[k, i, :, spans[h]] = wanted(k, dest, h)
                core_copy(k, i, h).start()

    def over_x(h):
        with scope(f"x{h}"):
            core_all(h).wait_recv()
            for k in range(own):
                for i in range(1, nx):
                    mine = wanted(k, (x + i) % nx * 2 + 1 - q, h)
                    sendb[k, i - 1, :, spans[h]] = mine + core_in[k, i, :, spans[h]]
                    xcopy(k, i, h).start()

    ids_copy.wait()
    to_core(0)

    @pl.when(q == 1)
    def _():
        over_x(0)

    for h in parts[1:]:
        to_core(h)
    int_copies = {}
    for k in range(own):
        cp = pltpu.make_async_copy(int_hbm.at[k], int_v.at[k].reshape(width, 2, ab), int_sem.at[k])
        cp.start()
        int_copies[k] = cp

    @pl.when(q == 1)
    def _():
        for h in parts[1:]:
            over_x(h)
    tail = (width // 128) * 128
    if padded > width:
        feed[:, tail:] = jnp.zeros((group, padded - tail), jnp.float32)

    def convert(k):
        int_copies[k].wait()
        whole = width // 16

        def split(at, count):
            for w in range(2):
                v = int_v[k, pl.ds(at * 2 + w, count, stride=2), :]
                h = v.astype(jnp.bfloat16)
                l = (v - h.astype(jnp.float32)).astype(jnp.bfloat16)
                if count < 16:
                    blank = jnp.zeros((16 - count, ab), jnp.bfloat16)
                    h = jnp.concatenate([h, blank], axis=0)
                    l = jnp.concatenate([l, blank], axis=0)
                hi[k, pl.ds(at, 16), w * ab:(w + 1) * ab] = h
                lo[k, pl.ds(at, 16), w * ab:(w + 1) * ab] = l

        def strip(i, carry):
            split(pl.multiple_of(i * 16, 16), 16)
            return carry

        lax.fori_loop(0, whole, strip, 0, unroll=4)
        done = whole * 16
        if width > done:
            split(done, width - done)
            done += 16
        if padded > done:
            hi[k, done:] = jnp.zeros((padded - done, 2 * ab), jnp.bfloat16)
            lo[k, done:] = jnp.zeros((padded - done, 2 * ab), jnp.bfloat16)

    def own_piece(k, h):
        total = wanted(k, c, h) + core_in[k, 0, :, spans[h]]
        for i in range(1, nx):
            xcopy(k, i, h).wait_recv()
            total = total + landed[k, i - 1, :, spans[h]]
        gath[k, y, z, :, spans[h]] = total
        if line:
            @pl.when(z == 3)
            def _():
                hop(k, h, z, 1).start()

            @pl.when(inner)
            def _():
                hop(k, h, z, facing).start()

            hop(k, h, z, pair).start()
            across(k, h, z).start()
        else:
            for d in range(1, nhi):
                hop(k, h, z, (z + d) % nhi).start()
            across(k, h, z).start()

    def relay(k, h, d):
        zz = order[d]
        hop(k, h, zz, z).wait_recv()
        if not line:
            across(k, h, zz).start()
            return
        if d == 1:
            @pl.when(inner)
            def _():
                hop(k, h, zz, pair).start()
        elif d == 2:
            @pl.when(z == 1)
            def _():
                hop(k, h, zz, facing).start()
        else:
            @pl.when(inner)
            def _():
                hop(k, h, zz, pair).start()

        if (k, h) in detour and d < 3:
            @pl.when(end if d == 2 else inner)
            def _():
                across(k, h, zz).start()
        else:
            across(k, h, zz).start()

    def pass_on(j):
        k, h = detour[j]
        gcopy(k, h, 1 - y, z, ys.at[h], gd.at[j], z * 2 + 1 - y).wait_recv()
        around(k, h).start()

    def multiply(k, h, acc):
        span = slice(spans[h].start, padded if h == last else spans[h].stop)
        for yy in range(2):
            for zz in range(nhi):
                at = (yy * nhi + zz) * rows
                feed[at:at + rows, spans[h]] = gath[k, yy, zz, :, spans[h]]
        f = feed[:, span]
        fh = f.astype(jnp.bfloat16)
        fl = (f - fh.astype(jnp.float32)).astype(jnp.bfloat16)
        both = jnp.concatenate([fh, fl], axis=0)
        big = jnp.dot(both, hi[k, span], preferred_element_type=jnp.float32)
        small = jnp.dot(fh, lo[k, span], preferred_element_type=jnp.float32)
        part = big[:group] + (big[group:] + small)
        return part if acc is None else acc + part

    @pl.when(q == 0)
    def _():
        with scope("cb"):
            for k in range(min(1, own)):
                convert(k)
        for h in parts:
            over_x(h)

    @pl.when(q == 1)
    def _():
        with scope("cb"):
            for k in range(min(2, own)):
                convert(k)


    acc = None
    for h in parts:
        for k in range(own):
            with scope(f"own{h}{k}"):
                own_piece(k, h)
    pieces = [(k, h) for h in parts for k in range(own)]
    with scope("cm"):
        for k in range(0, min(0 + 0, own)):
            convert(k)
    if line:
        @pl.when(inner)
        def _():
            steps = [(j + (0, -3, 3)[d - 1], d, j) for j in range(len(pieces)) for d in range(1, nhi)]
            steps += [(14 + i, nhi, i) for i in range(len(detour))]
            for _, d, j in sorted(steps):
                with scope(f"i{d}_{j}"):
                    if d == nhi:
                        pass_on(j)
                    else:
                        relay(*pieces[j], d)

        @pl.when(end)
        def _():
            steps = [(j, 1, j) for j in range(len(pieces))]
            steps += [(0 + i, 4, i) for i in range(len(detour))]
            for _, d, j in sorted(steps):
                with scope(f"e{d}_{j}"):
                    if d == nhi:
                        pass_on(j)
                    else:
                        relay(*pieces[j], 1)
    else:
        for k, h in pieces:
            for d in range(1, nhi):
                relay(k, h, d)
    with scope("cc"):
        for k in range(1, min(2, own)):
            @pl.when(q == 0)
            def _():
                convert(k)

        for k in range(2, own):
            convert(k)

    def product(j, acc):
        k, h = pieces[j]
        with scope(f"w{h}{k}"):
            many(nhi - ((k, h) in detour), h, ys.at[h], fill(k, h)).wait_recv()
        with scope(f"q{h}{k}"):
            return multiply(k, h, acc)

    ready = 0
    for n in range(len(pieces) + 1):
        if line:
            @pl.when(end)
            def _():
                if n < len(pieces):
                    with scope(f"e2_{n}"):
                        relay(*pieces[n], 2)
                if n >= 1:
                    with scope(f"e3_{n-1}"):
                        relay(*pieces[n - 1], 3)

        if n == 1 + 1:
            with scope("sends"):
                mirror_copy.wait()
                for h in parts:
                    core_all(h).wait_send()
                    pltpu.make_async_remote_copy(
                        src_ref=sendb.at[:, :, :, spans[h]], dst_ref=landed.at[:, :, :, spans[h]],
                        send_sem=xs.at[h], recv_sem=xr.at[h, 0, 0],
                        device_id=(b, (x + 1) % nx * 2 + q), device_id_type=MESH).wait_send()
        if n >= 1 + 5 and n < len(pieces) + 1 - 1:
            acc = product(ready, acc)
            ready += 1
    for j in range(ready, len(pieces)):
        acc = product(j, acc)

    deep = group // 4
    for yy in range(2):
        first = acc[2 * yy * deep:(2 * yy + 1) * deep]
        second = acc[(2 * yy + 1) * deep:(2 * yy + 2) * deep]
        sums = first[:, :ab] + second[:, :ab]
        diffs = first[:, ab:] - second[:, ab:]
        swapped = 0.5 * (sums - diffs)
        direct = 0.5 * (sums + diffs)
        for zz in range(nhi // 2):
            at = (zz * 2 + yy) * rows
            swp[0, at:at + rows] = direct[zz * rows:(zz + 1) * rows]
            swp[1, at:at + rows] = swapped[zz * rows:(zz + 1) * rows]
    for g in range(ncol):
        for i in range(own_pairs):
            p = g * own_pairs + i
            osend[g, i:i + 1, :] = swp[0, p:p + 1] + swp[1, pl.ds(mirror[p], 1), :]

    def ocopy(j):
        return pltpu.make_async_remote_copy(
            src_ref=osend.at[(c + j) % ncol], dst_ref=orecv.at[j - 1],
            send_sem=os_.at[0], recv_sem=or_.at[0],
            device_id=(b, (c + j) % ncol), device_id_type=MESH)

    for j in range(1, ncol):
        ocopy(j).start()
    with scope("sends2"):
        for h in parts:
            gone = len([j for j in detour if j[1] == h])
            many(own * nhi - gone, h, ys.at[h], gy.at[0, 0]).wait_send()
            if line:
                for layer, count in ((0, own), (1, 5 * own), (2, 4 * own), (3, 2 * own)):
                    @pl.when(z == layer)
                    def _():
                        many(count + gone, h, zs.at[h], gy.at[0, 0]).wait_send()
            else:
                many(own * (nhi - 1), h, zs.at[h], gy.at[0, 0]).wait_send()
    total = osend[c]
    with scope("owait"):
        every = pltpu.make_async_remote_copy(
            src_ref=orecv, dst_ref=orecv, send_sem=os_.at[0], recv_sem=or_.at[0],
            device_id=(b, (c + 1) % ncol), device_id_type=MESH)
        every.wait_recv()
    for j in range(1, ncol):
        total = total + orecv[j - 1]
    out_ref[...] = total
    every.wait_send()


def chunks(width):
    middle = width // 2 // 256 * 256
    return (slice(0, middle), slice(middle, width)) if middle else (slice(0, width),)


def body(nblk, ncol, amplitudes, integrals, block_ids, mirror):
    blocks_here, rows, width = amplitudes.shape
    _, ab, own, _ = integrals.shape
    pairs = mirror.shape[0]
    own_pairs = pairs // ncol
    padded = -(-width // 128) * 128
    nhi = nblk // 2
    nx = ncol // 2
    f32 = jnp.float32
    dma = pltpu.SemaphoreType.DMA
    parts = len(chunks(width))
    return pl.pallas_call(
        functools.partial(kernel, nblk, ncol),
        out_shape=pltpu.VMEM((own_pairs, ab), f32),
        in_specs=[pl.BlockSpec(memory_space=pl.ANY)] * 4,
        out_specs=pl.BlockSpec(memory_space=pltpu.VMEM),
        scratch_shapes=[
            tuple(pltpu.VMEM((blocks_here, rows, s.stop - s.start), f32) for s in chunks(width)),
            pltpu.VMEM((own, 2 * width, ab), f32),
            pltpu.VMEM((own, padded, 2 * ab), jnp.bfloat16),
            pltpu.VMEM((own, padded, 2 * ab), jnp.bfloat16),
            pltpu.VMEM((own, nx, rows, width), f32),
            pltpu.VMEM((own, nx, rows, width), f32),
            pltpu.VMEM((own, nx - 1, rows, width), f32),
            pltpu.VMEM((own, nx - 1, rows, width), f32),
            pltpu.VMEM((own, 2, nhi, rows, width), f32),
            pltpu.VMEM((2 * nhi * rows, padded), f32),
            pltpu.VMEM((2, pairs, ab), f32),
            pltpu.VMEM((ncol, own_pairs, ab), f32),
            pltpu.VMEM((ncol - 1, own_pairs, ab), f32),
            pltpu.SMEM(block_ids.shape, jnp.int32),
            pltpu.SMEM(mirror.shape, jnp.int32),
            dma((parts,)),
            dma((own,)),
            dma((2,)),
            dma((parts,)),
            dma((parts,)),
            dma((parts,)),
            dma((parts, own, nx - 1)),
            dma((parts,)),
            dma((parts,)),
            dma((parts, own, nhi - 1)),
            dma((1,)),
            dma((parts, own)),
            dma((1,)),
            dma((1,)),
        ],
        compiler_params=pltpu.CompilerParams(
            collective_id=0, has_side_effects=True, vmem_limit_bytes=60 * 1024 * 1024
        ),
    )(amplitudes, jnp.transpose(integrals, (2, 3, 0, 1)), block_ids, mirror)


def solution(mesh):
    in_specs = (P("col", "blk", None), P(None, "blk", "col", None), P(), P())
    out_specs = P("col", "blk")
    call = functools.partial(body, mesh.shape["blk"], mesh.shape["col"])
    return jax.shard_map(call, mesh=mesh, in_specs=in_specs, out_specs=out_specs, check_vma=False)
```

time: 28.5 us -> 26.3 us (0.923)
  Pallas kernels: 27.8 us -> 25.6 us
    pallas_call x1, Pallas kernels: 27.8 us -> 25.6 us  [body(): pl.pallas_call(functools.partial(kernel, nblk, ncol), out_shape=pltpu.VME...]
where the time goes in v2:
time: 26.3 us; the launch traced here: 26.2 us
  Pallas kernels  25.6 us (97%)
  local copies, waits for them, and re-layouts  0.58 us (2%)
    pallas_call x1, Pallas kernels, body(): pl.pallas_call(functools.partial(kernel, nblk, ncol), out_shape=pltpu.VME...  25.6 us
    unnamed x1, local copies, waits for them, and re-layouts  0.58 us

profile of v2, /device:TPU:0, one launch (start us, length us, event | category | flops | bytes accessed | tf_op | source)
XLA Modules:
  0.0 26.2 jit_solution(13836504815729982464)
XLA Ops:
  0.0 25.6 %shard_map.46 = f32[4,128]{1,0:T(4,128)S(1)} custom-call(f32[200,4,1601]{2,1,0:T(4,128)} %amp_hbm.1, f32[5,1601,2,128]{3,2,1,0:T(2,128)} %bitcast.1, s32[20]{0:T(128)} %ids_hbm.1, s32[16]{0:T(128)} %mirror_hbm.1), custom_call_target="tpu_custom_call" | custom-call | tf_op jit(solution)/shard_map/pallas_call | solution.py:432
  25.6 0.6 %copy.6 = f32[4,128]{1,0:T(4,128)} copy(f32[4,128]{1,0:T(4,128)S(1)} %shard_map.46) | data formatting | bytes 4096

commit v3 on v2

--- a/solution.py
+++ b/solution.py
@@ -76,7 +76,11 @@
             def _():
                 greet((3 * 2 + y, c))
 
-            pl.semaphore_wait(barrier, ncol + 2 - (z == 0).astype(jnp.int32))
+            @pl.when(z == 0)
+            def _():
+                greet((2 * 2 + y, c))
+
+            pl.semaphore_wait(barrier, ncol + 2 - (z == 0).astype(jnp.int32) + (z == 2).astype(jnp.int32))
         else:
             for d in range(1, nhi):
                 greet((order[d] * 2 + y, c))
@@ -215,11 +219,18 @@
             def _():
                 hop(k, h, z, 1).start()
 
-            @pl.when(inner)
+            @pl.when(z == 2)
+            def _():
+                hop(k, h, z, 0).start()
+
+            @pl.when(z == 1)
             def _():
                 hop(k, h, z, facing).start()
 
-            hop(k, h, z, pair).start()
+            @pl.when(z != 3)
+            def _():
+                hop(k, h, z, pair).start()
+
             across(k, h, z).start()
         else:
             for d in range(1, nhi):
@@ -233,7 +244,7 @@
             across(k, h, zz).start()
             return
         if d == 1:
-            @pl.when(inner)
+            @pl.when(z == 2)
             def _():
                 hop(k, h, zz, pair).start()
         elif d == 2:
@@ -296,40 +307,50 @@
     with scope("cm"):
         for k in range(0, min(0 + 0, own)):
             convert(k)
+
     if line:
-        @pl.when(inner)
+        @pl.when(z == 3)
         def _():
-            steps = [(j + (0, -3, 3)[d - 1], d, j) for j in range(len(pieces)) for d in range(1, nhi)]
-            steps += [(14 + i, nhi, i) for i in range(len(detour))]
-            for _, d, j in sorted(steps):
-                with scope(f"i{d}_{j}"):
-                    if d == nhi:
-                        pass_on(j)
-                    else:
+            for k, h in pieces:
+                hop(k, h, z, pair).start()
+
+        @pl.when(z == 2)
+        def _():
+            for k, h in pieces:
+                hop(k, h, z, facing).start()
+
+    with scope("cc"):
+        for k in range(1, min(2, own)):
+            @pl.when(q == 0)
+            def _():
+                convert(k)
+
+        for k in range(2, own):
+            convert(k)
+
+
+    if line:
+        pass
+
+        for layer, lags in ((1, (12, -3, 0)), (2, (0, 1, 4))):
+            @pl.when(z == layer)
+            def _():
+                for _, d, j in sorted((j + lags[d - 1], d, j) for j in range(len(pieces)) for d in range(1, nhi)):
+                    with scope(f"i{d}_{j}"):
                         relay(*pieces[j], d)
 
         @pl.when(end)
         def _():
-            steps = [(j, 1, j) for j in range(len(pieces))]
-            steps += [(0 + i, 4, i) for i in range(len(detour))]
-            for _, d, j in sorted(steps):
-                with scope(f"e{d}_{j}"):
-                    if d == nhi:
-                        pass_on(j)
-                    else:
-                        relay(*pieces[j], 1)
+            for j in range(len(pieces)):
+                with scope(f"e1_{j}"):
+                    relay(*pieces[j], 1)
+            for j in range(0):
+                with scope(f"e2_{j}"):
+                    relay(*pieces[j], 2)
     else:
         for k, h in pieces:
             for d in range(1, nhi):
                 relay(k, h, d)
-    with scope("cc"):
-        for k in range(1, min(2, own)):
-            @pl.when(q == 0)
-            def _():
-                convert(k)
-
-        for k in range(2, own):
-            convert(k)
 
     def product(j, acc):
         k, h = pieces[j]
@@ -338,28 +359,28 @@
         with scope(f"q{h}{k}"):
             return multiply(k, h, acc)
 
+    mirror_copy.wait()
+    for h in parts:
+        core_all(h).wait_send()
+        pltpu.make_async_remote_copy(
+            src_ref=sendb.at[:, :, :, spans[h]], dst_ref=landed.at[:, :, :, spans[h]],
+            send_sem=xs.at[h], recv_sem=xr.at[h, 0, 0],
+            device_id=(b, (x + 1) % nx * 2 + q), device_id_type=MESH).wait_send()
+
+    steps = sorted((j + (0, 10, 12)[d - 1], d, j) for j in range(len(pieces)) for d in (2, 3))
+    last3 = [n for n, s in enumerate(steps) if s[1] == 3]
     ready = 0
-    for n in range(len(pieces) + 1):
+    at = 0
+    for j in range(len(pieces)):
+        stop = last3[j] + 1
         if line:
             @pl.when(end)
             def _():
-                if n < len(pieces):
-                    with scope(f"e2_{n}"):
-                        relay(*pieces[n], 2)
-                if n >= 1:
-                    with scope(f"e3_{n-1}"):
-                        relay(*pieces[n - 1], 3)
-
-        if n == 1 + 1:
-            with scope("sends"):
-                mirror_copy.wait()
-                for h in parts:
-                    core_all(h).wait_send()
-                    pltpu.make_async_remote_copy(
-                        src_ref=sendb.at[:, :, :, spans[h]], dst_ref=landed.at[:, :, :, spans[h]],
-                        send_sem=xs.at[h], recv_sem=xr.at[h, 0, 0],
-                        device_id=(b, (x + 1) % nx * 2 + q), device_id_type=MESH).wait_send()
-        if n >= 1 + 5 and n < len(pieces) + 1 - 1:
+                for _, d, i in steps[at:stop]:
+                    with scope(f"e{d}_{i}"):
+                        relay(*pieces[i], d)
+        at = stop
+        if 9 <= j < len(pieces) - 1:
             acc = product(ready, acc)
             ready += 1
     for j in range(ready, len(pieces)):
@@ -395,7 +416,7 @@
             gone = len([j for j in detour if j[1] == h])
             many(own * nhi - gone, h, ys.at[h], gy.at[0, 0]).wait_send()
             if line:
-                for layer, count in ((0, own), (1, 5 * own), (2, 4 * own), (3, 2 * own)):
+                for layer, count in ((0, own), (1, 4 * own), (2, 5 * own), (3, 2 * own)):
                     @pl.when(z == layer)
                     def _():
                         many(count + gone, h, zs.at[h], gy.at[0, 0]).wait_send()

time: 26.3 us -> 26.2 us (level)
  no operation moved by 1% of the time
where the time goes in v3:
time: 26.2 us; the launch traced here: 26.1 us
  Pallas kernels  25.5 us (97%)
  local copies, waits for them, and re-layouts  0.58 us (2%)
    pallas_call x1, Pallas kernels, body(): pl.pallas_call(functools.partial(kernel, nblk, ncol), out_shape=pltpu.VME...  25.5 us
    unnamed x1, local copies, waits for them, and re-layouts  0.58 us

profile of v3, /device:TPU:0, one launch (start us, length us, event | category | flops | bytes accessed | tf_op | source)
XLA Modules:
  0.0 26.1 jit_solution(12110093201345342140)
XLA Ops:
  0.0 25.5 %shard_map.46 = f32[4,128]{1,0:T(4,128)S(1)} custom-call(f32[200,4,1601]{2,1,0:T(4,128)} %amp_hbm.1, f32[5,1601,2,128]{3,2,1,0:T(2,128)} %bitcast.1, s32[20]{0:T(128)} %ids_hbm.1, s32[16]{0:T(128)} %mirror_hbm.1), custom_call_target="tpu_custom_call" | custom-call | tf_op jit(solution)/shard_map/pallas_call | solution.py:453
  25.5 0.6 %copy.6 = f32[4,128]{1,0:T(4,128)} copy(f32[4,128]{1,0:T(4,128)S(1)} %shard_map.46) | data formatting | bytes 4096

commit v4 on v3

--- a/solution.py
+++ b/solution.py
@@ -15,7 +15,7 @@
     nblk, ncol,
     amp_hbm, int_hbm, ids_hbm, mirror_hbm, out_ref,
     amp_v, int_v, hi, lo, core_out, core_in, sendb, landed, gath, feed, swp, osend, orecv, ids, mirror,
-    amp_sem, int_sem, tab_sem, cs, cr, xs, xr, zs, ys, gz, gd, gy, os_, or_,
+    amp_sem, int_sem, tab_sem, cr, xr, ss, gz, gy, os_, or_,
 ):
     blocks_here, rows, width = amp_hbm.shape
     own, _, ab = int_v.shape
@@ -41,10 +41,8 @@
     inner = jnp.logical_not(end)
     if line:
         order = (z, jnp.where(end, pair, facing), jnp.where(end, cross, pair), jnp.where(end, facing, cross))
-        detour = ()
     else:
         order = tuple((z + nhi - d) % nhi for d in range(nhi))
-        detour = ()
 
     ids_copy = pltpu.make_async_copy(ids_hbm, ids, tab_sem.at[0])
     mirror_copy = pltpu.make_async_copy(mirror_hbm, mirror, tab_sem.at[1])
@@ -89,19 +87,19 @@
     def core_copy(k, i, h):
         return pltpu.make_async_remote_copy(
             src_ref=core_out.at[k, i, :, spans[h]], dst_ref=core_in.at[k, i, :, spans[h]],
-            send_sem=cs.at[h], recv_sem=cr.at[h],
+            send_sem=ss.at[h], recv_sem=cr.at[h],
             device_id=(b, x * 2 + 1 - q), device_id_type=MESH)
 
     def core_all(h):
         return pltpu.make_async_remote_copy(
             src_ref=core_out.at[:, :, :, spans[h]], dst_ref=core_in.at[:, :, :, spans[h]],
-            send_sem=cs.at[h], recv_sem=cr.at[h],
+            send_sem=ss.at[h], recv_sem=cr.at[h],
             device_id=(b, x * 2 + 1 - q), device_id_type=MESH)
 
     def xcopy(k, i, h):
         return pltpu.make_async_remote_copy(
             src_ref=sendb.at[k, i - 1, :, spans[h]], dst_ref=landed.at[k, i - 1, :, spans[h]],
-            send_sem=xs.at[h], recv_sem=xr.at[h, k, i - 1],
+            send_sem=ss.at[h], recv_sem=xr.at[h, k, i - 1],
             device_id=(b, (x + i) % nx * 2 + 1 - q), device_id_type=MESH)
 
     def gcopy(k, h, yy, zz, send, recv, target):
@@ -110,19 +108,11 @@
             src_ref=piece, dst_ref=piece, send_sem=send, recv_sem=recv,
             device_id=(target, c), device_id_type=MESH)
 
-    def fill(k, h):
-        return gy.at[h, k]
-
     def across(k, h, zz):
-        early = (k, h) in detour and zz is z
-        recv = gd.at[detour.index((k, h))] if early else fill(k, h)
-        return gcopy(k, h, y, zz, ys.at[h], recv, z * 2 + 1 - y)
+        return gcopy(k, h, y, zz, ss.at[h], gy.at[h, k], z * 2 + 1 - y)
 
     def hop(k, h, zsrc, zdst):
-        return gcopy(k, h, y, zsrc, zs.at[h], gz.at[h, k, (zsrc + nhi - zdst) % nhi - 1], zdst * 2 + y)
-
-    def around(k, h):
-        return gcopy(k, h, 1 - y, z, zs.at[h], fill(k, h), pair * 2 + y)
+        return gcopy(k, h, y, zsrc, ss.at[h], gz.at[h, k, (zsrc + nhi - zdst) % nhi - 1], zdst * 2 + y)
 
     def many(count, h, send, recv):
         piece = gath.reshape(own * nblk, rows, width).at[0:count, :, spans[h]]
@@ -256,17 +246,7 @@
             def _():
                 hop(k, h, zz, pair).start()
 
-        if (k, h) in detour and d < 3:
-            @pl.when(end if d == 2 else inner)
-            def _():
-                across(k, h, zz).start()
-        else:
-            across(k, h, zz).start()
-
-    def pass_on(j):
-        k, h = detour[j]
-        gcopy(k, h, 1 - y, z, ys.at[h], gd.at[j], z * 2 + 1 - y).wait_recv()
-        around(k, h).start()
+        across(k, h, zz).start()
 
     def multiply(k, h, acc):
         span = slice(spans[h].start, padded if h == last else spans[h].stop)
@@ -355,18 +335,11 @@
     def product(j, acc):
         k, h = pieces[j]
         with scope(f"w{h}{k}"):
-            many(nhi - ((k, h) in detour), h, ys.at[h], fill(k, h)).wait_recv()
+            many(nhi, h, ss.at[h], gy.at[h, k]).wait_recv()
         with scope(f"q{h}{k}"):
             return multiply(k, h, acc)
 
     mirror_copy.wait()
-    for h in parts:
-        core_all(h).wait_send()
-        pltpu.make_async_remote_copy(
-            src_ref=sendb.at[:, :, :, spans[h]], dst_ref=landed.at[:, :, :, spans[h]],
-            send_sem=xs.at[h], recv_sem=xr.at[h, 0, 0],
-            device_id=(b, (x + 1) % nx * 2 + q), device_id_type=MESH).wait_send()
-
     steps = sorted((j + (0, 10, 12)[d - 1], d, j) for j in range(len(pieces)) for d in (2, 3))
     last3 = [n for n, s in enumerate(steps) if s[1] == 3]
     ready = 0
@@ -412,16 +385,20 @@
     for j in range(1, ncol):
         ocopy(j).start()
     with scope("sends2"):
-        for h in parts:
-            gone = len([j for j in detour if j[1] == h])
-            many(own * nhi - gone, h, ys.at[h], gy.at[0, 0]).wait_send()
-            if line:
-                for layer, count in ((0, own), (1, 4 * own), (2, 5 * own), (3, 2 * own)):
-                    @pl.when(z == layer)
-                    def _():
-                        many(count + gone, h, zs.at[h], gy.at[0, 0]).wait_send()
-            else:
-                many(own * (nhi - 1), h, zs.at[h], gy.at[0, 0]).wait_send()
+        def sent(count):
+            for h in parts:
+                for at in range(0, count, blocks_here):
+                    some = amp_v[h].at[0:min(blocks_here, count - at)]
+                    pltpu.make_async_copy(some, some, ss.at[h]).wait()
+
+        local = own * (2 * nx - 1) + own * nhi
+        if line:
+            for layer, count in enumerate((own, 4 * own, 5 * own, 2 * own)):
+                @pl.when(z == layer)
+                def _():
+                    sent(local + count)
+        else:
+            sent(local + own * (nhi - 1))
     total = osend[c]
     with scope("owait"):
         every = pltpu.make_async_remote_copy(
@@ -475,13 +452,9 @@
             dma((own,)),
             dma((2,)),
             dma((parts,)),
-            dma((parts,)),
-            dma((parts,)),
             dma((parts, own, nx - 1)),
             dma((parts,)),
-            dma((parts,)),
             dma((parts, own, nhi - 1)),
-            dma((1,)),
             dma((parts, own)),
             dma((1,)),
             dma((1,)),

time: 26.2 us -> 26.1 us (level)
  no operation moved by 1% of the time
where the time goes in v4:
time: 26.1 us; the launch traced here: 26 us
  Pallas kernels  25.4 us (97%)
  local copies, waits for them, and re-layouts  0.58 us (2%)
    pallas_call x1, Pallas kernels, body(): pl.pallas_call(functools.partial(kernel, nblk, ncol), out_shape=pltpu.VME...  25.4 us
    unnamed x1, local copies, waits for them, and re-layouts  0.58 us

profile of v4, /device:TPU:0, one launch (start us, length us, event | category | flops | bytes accessed | tf_op | source)
XLA Modules:
  0.0 26.0 jit_solution(1011972529498416052)
XLA Ops:
  0.0 25.4 %shard_map.46 = f32[4,128]{1,0:T(4,128)S(1)} custom-call(f32[200,4,1601]{2,1,0:T(4,128)} %amp_hbm.1, f32[5,1601,2,128]{3,2,1,0:T(2,128)} %bitcast.1, s32[20]{0:T(128)} %ids_hbm.1, s32[16]{0:T(128)} %mirror_hbm.1), custom_call_target="tpu_custom_call" | custom-call | tf_op jit(solution)/shard_map/pallas_call | solution.py:430
  25.4 0.6 %copy.6 = f32[4,128]{1,0:T(4,128)} copy(f32[4,128]{1,0:T(4,128)S(1)} %shard_map.46) | data formatting | bytes 4096

commit v5 on v3

--- a/solution.py
+++ b/solution.py
@@ -380,7 +380,7 @@
                     with scope(f"e{d}_{i}"):
                         relay(*pieces[i], d)
         at = stop
-        if 9 <= j < len(pieces) - 1:
+        if 10 <= j < len(pieces) - 1:
             acc = product(ready, acc)
             ready += 1
     for j in range(ready, len(pieces)):

time: 26.2 us -> 26.2 us (level)
  no operation moved by 1% of the time
where the time goes in v5:
time: 26.2 us; the launch traced here: 26.1 us
  Pallas kernels  25.5 us (97%)
  local copies, waits for them, and re-layouts  0.58 us (2%)
    pallas_call x1, Pallas kernels, body(): pl.pallas_call(functools.partial(kernel, nblk, ncol), out_shape=pltpu.VME...  25.5 us
    unnamed x1, local copies, waits for them, and re-layouts  0.58 us

profile of v5, /device:TPU:0, one launch (start us, length us, event | category | flops | bytes accessed | tf_op | source)
XLA Modules:
  0.0 26.1 jit_solution(12110093201345342140)
XLA Ops:
  0.0 25.5 %shard_map.46 = f32[4,128]{1,0:T(4,128)S(1)} custom-call(f32[200,4,1601]{2,1,0:T(4,128)} %amp_hbm.1, f32[5,1601,2,128]{3,2,1,0:T(2,128)} %bitcast.1, s32[20]{0:T(128)} %ids_hbm.1, s32[16]{0:T(128)} %mirror_hbm.1), custom_call_target="tpu_custom_call" | custom-call | tf_op jit(solution)/shard_map/pallas_call | solution.py:453
  25.5 0.6 %copy.6 = f32[4,128]{1,0:T(4,128)} copy(f32[4,128]{1,0:T(4,128)S(1)} %shard_map.46) | data formatting | bytes 4096
